TPU v7x, 32 devices: a whole 2x2x4 slice. The times are simulated.
32 devices in a mesh: col: 4 (over z), row: 8 (over y, x, core).
Axes of the slice: x: 2, y: 2, z: 4, core: 2. Of those that a mesh axis runs over, the one named last changes fastest.
Arguments:
- affinity: bfloat16 [3840, 128, 128], P(('col', 'row')), may hold values from 0 to 0.015625
- tile_rows: int32 [3840], P(('col', 'row')), may hold values from 0 to 19
- tile_cols: int32 [3840], P(('col', 'row')), may hold values from 0 to 39
- live_tiles: int32 [32], P(('col', 'row')), may hold values from 1 to 120, as said below
- start: float32 [20480, 256], P(('col', 'row')), may hold values from -1500 to 1500
Outputs:
- vectors: float32 [20480, 256], P(('col', 'row'))
- first_passes: float32 [2, 20480, 256], P(None, ('col', 'row'))
Inputs may be any that keep to these rules, and one draw needn't show every extreme that they name: A device's tiles are its slots 0 to live_tiles - 1; later slots are ignored. Some device holds exactly 120 tiles.
All inputs are finite; a program needn't handle non-finite values.
Results may differ from a plain program's by a relative error of at most 0.0003.
Values sent between devices are 32-bit elements; how exact they have to be, the bound alone decides.
No kernel may reach another device: no remote copies, remote signals or barrier semaphores. Data moves between devices by JAX's collectives and lax.ppermute only.
A program may use at most 128 MiB of HBM per device.

v0:
```python
import jax
import jax.numpy as jnp
from jax import lax
from jax.sharding import PartitionSpec as P

ITERS = 2
highest = lax.Precision.HIGHEST


def local_gram(matrix):
    return jnp.dot(matrix.T, matrix, precision=highest, preferred_element_type=jnp.float32)


def inverse_lower(gram):
    lower = jnp.linalg.cholesky(gram)
    return jax.scipy.linalg.solve_triangular(
        lower, jnp.eye(gram.shape[0], dtype=jnp.float32), lower=True
    )


def apply_factor(matrix, inverse):
    return jnp.dot(matrix, inverse.T, precision=highest, preferred_element_type=jnp.float32)


def body(affinity, tile_rows, tile_cols, live_tiles, start):
    n_row = lax.axis_size("row")
    n_col = lax.axis_size("col")
    slot_count = affinity.shape[0]
    tile_size = affinity.shape[1]
    rows_local = start.shape[0]
    vec_count = start.shape[1]
    own_tiles = rows_local // tile_size
    live = (jnp.arange(slot_count) < live_tiles[0]).astype(jnp.float32)
    row_onehot = (jnp.arange(own_tiles * n_col)[:, None] == tile_rows[None, :]).astype(
        jnp.float32
    ) * live[None, :]
    row_sums = jnp.sum(affinity, axis=2, dtype=jnp.float32)
    degree_terms = jnp.dot(
        row_onehot, row_sums, precision=highest, preferred_element_type=jnp.float32
    )
    degree = 1.0 + lax.psum_scatter(degree_terms, "col", scatter_dimension=0, tiled=True).reshape(
        rows_local
    )
    scaling = (1.0 / jnp.sqrt(degree))[:, None]
    squares = affinity.astype(jnp.float32)
    firsts = []
    pending = start
    for step_number in range(ITERS):
        mapped_scaled = scaling * pending
        gathered = lax.all_gather(mapped_scaled, "row", axis=0, tiled=True)
        gathered = gathered.reshape(n_row * own_tiles, tile_size, vec_count)
        picked = gathered[tile_cols]
        products = jnp.einsum(
            "sij,sjk->sik", squares, picked, precision=highest, preferred_element_type=jnp.float32
        )
        terms = jnp.dot(
            row_onehot,
            products.reshape(slot_count, tile_size * vec_count),
            precision=highest,
            preferred_element_type=jnp.float32,
        )
        summed = lax.psum_scatter(terms, "col", scatter_dimension=0, tiled=True)
        raw_image = scaling * (mapped_scaled + summed.reshape(rows_local, vec_count))
        if step_number == 0:
            inner_gram = lax.psum(local_gram(raw_image), ("col", "row"))
            image_block = raw_image
        else:
            raw_gram, pending_gram = lax.psum(
                (local_gram(raw_image), local_gram(pending)), ("col", "row")
            )
            pending_inverse = inverse_lower(pending_gram)
            image_block = apply_factor(raw_image, pending_inverse)
            inner_gram = jnp.dot(
                jnp.dot(
                    pending_inverse, raw_gram, precision=highest, preferred_element_type=jnp.float32
                ),
                pending_inverse.T,
                precision=highest,
                preferred_element_type=jnp.float32,
            )
        pending = apply_factor(image_block, inverse_lower(inner_gram))
        firsts.append(pending)
    final_gram = lax.psum(local_gram(pending), ("col", "row"))
    basis = apply_factor(pending, inverse_lower(final_gram))
    total_images = rows_local * n_row * n_col
    root = jnp.sqrt(jnp.float32(total_images))
    return (root * basis, root * jnp.stack(firsts, axis=0))


def solution(mesh):
    placed = (
        P(("col", "row"), None, None),
        P(("col", "row")),
        P(("col", "row")),
        P(("col", "row")),
        P(("col", "row"), None),
    )
    return jax.shard_map(
        body,
        mesh=mesh,
        in_specs=placed,
        out_specs=(P(("col", "row"), None), P(None, ("col", "row"), None)),
        check_vma=False,
    )
```

profile of v0, /device:TPU:0, one launch (start us, length us, event | category | flops | bytes accessed | tf_op | source)
XLA Modules:
  0.0 1157.0 jit_solution(773065271221598994)
XLA Ops:
  7.9 3.2 convert_reduce_fusion
  11.9 20.4 %all-reduce.1 = f32[20,128]{1,0:T(8,128)S(1)} all-reduce(f32[20,128]{1,0:T(8,128)S(1)} %fusion.55), channel_id=2, replica_groups=mesh['col'=4,'row'=8] {'col'}, use_global_device_ids=true, to_apply=%region_1.0.clone | all-reduce | flops 2560 | bytes 20480
  34.4 2.1 broadcast_multiply_fusion.1
  36.6 39.3 %all-gather.3.cloned.1.call-done = f32[5120,256]{1,0:T(8,128)} async-done(((f32[640,256]{1,0:T(8,128)}), f32[5120,256]{1,0:T(8,128)}) %all-gather.3.cloned.1.call-update) | async-done | bytes 5242896 | tf_op jit(solution)/shard_map/all_gather | solution.py:50
  75.9 12.1 %gather_fusion = f32[120,128,256]{2,1,0:T(8,128)} fusion(f32[40,128,256]{2,1,0:T(8,128)} %bitcast.166, s32[1024]{0:T(1024)S(1)} %pad_clamp_fusion), kind=kCustom, calls=%fused_computation | custom fusion | bytes 31457760 | tf_op jit(solution)/shard_map/gather | solution.py:52
  88.0 20.2 %convolution_bitcast_fusion.1 = f32[120,128,256]{1,2,0:T(8,128)} fusion(f32[120,128,256]{2,1,0:T(8,128)} %gather_fusion, bf16[120,128,128]{2,1,0:T(8,128)(2,1)} %param.8), kind=kOutput, calls=%fused_computation.11 | convolution fusion | flops 6039797760 | bytes 35389440 | tf_op jit(solution)/shard_map/sij,sjk->sik/dot_general | solution.py:53
  108.2 15.7 %copy.41 = f32[15,8,128,256]{3,1,2,0:T(8,128)} copy(f32[15,8,128,256]{2,3,1,0:T(8,128)} %bitcast.163) | data formatting | bytes 31457280
  123.9 10.5 fusion.53
  134.4 78.5 %fusion = f32[8,32768]{1,0:T(8,128)} fusion(f32[20,32768]{1,0:T(8,128)S(1)} %fusion.53), kind=kCustom, calls=%all-reduce-scatter | all-reduce-scatter fusion | flops 1048577 | bytes 3670528
  215.7 2.6 collective-permute-start.1
  219.0 20.1 %collective-permute-done.1 = f32[1,32768]{1,0:T(1,128)S(1)} collective-permute-done((f32[1,32768]{1,0:T(1,128)S(1)}, f32[1,32768]{1,0:T(1,128)S(1)}, u32[]{:S(2)}, u32[]{:S(2)}) %collective-permute-start.1) | collective-permute-done | bytes 131104
  239.1 21.2 %concatenate.3 = f32[17,32768]{1,0:T(8,128)} concatenate(f32[1,32768]{1,0:T(1,128)S(1)} %collective-permute-done.1, f32[8,32768]{1,0:T(8,128)S(1)} %collective-permute-done, f32[8,32768]{1,0:T(8,128)} %fusion), dimensions={0} | concatenate | bytes 4456448
  262.4 2.2 fusion.29
  264.6 129.0 %all-reduce.11.cloned.1.call-done = f32[256,256]{0,1:T(8,128)} async-done(((f32[256,256]{0,1:T(8,128)}), f32[256,256]{0,1:T(8,128)}) %all-reduce.11.cloned.1.call-update) | async-done | bytes 262160 | tf_op jit(solution)/shard_map/psum | solution.py:65
  395.7 11.7 %cholesky.214 = f32[128,128]{1,0:T(8,128)S(1)} custom-call(f32[128,128]{1,0:T(8,128)S(1)} %cholesky.346), custom_call_target="Cholesky" | custom-call | tf_op jit(solution)/shard_map/jit(cholesky)/cholesky | solution.py:15
  407.5 9.8 custom-call.17
  417.8 11.7 %cholesky.231 = f32[128,128]{1,0:T(8,128)S(1)} custom-call(f32[128,128]{1,0:T(8,128)S(1)} %convolution_subtract_fusion.7), custom_call_target="Cholesky" | custom-call | tf_op jit(solution)/shard_map/jit(cholesky)/cholesky | solution.py:15
  431.8 15.1 %while.8 = (s32[]{:T(128)}, f32[256,256]{1,0:T(8,128)S(1)}, s32[2,2]{1,0:T(2,128)S(1)}, f32[2,128,128]{2,1,0:T(8,128)S(1)}, s32[]{:T(128)}) while((s32[]{:T(128)}, f32[256,256]{1,0:T(8,128)S(1)}, s32[2,2]{1,0:T(2,128)S(1)}, f32[2,128,128]{2,1,0:T(8,128)S(1)}, s32[]{:T(128)}) %tuple.83), condition=%wide.while_cond, body=%wide.while_body.sunk | while | flops 2 | bytes 131181 | solution.py:16
  446.9 19.7 %custom-call.18 = f32[2,128,128]{1,2,0:T(8,128)S(1)} custom-call(f32[2,128,128]{2,1,0:T(8,128)S(1)} %get-tuple-element.30), custom_call_target="InvertDiagBlocksLowerTriangular" | custom-call | tf_op jit(solution)/shard_map/jit(_solve_triangular)/triangular_solve | solution.py:16
  469.1 40.2 %all-gather.5.cloned.1.call-done = f32[5120,256]{1,0:T(8,128)} async-done(((f32[640,256]{1,0:T(8,128)}), f32[5120,256]{1,0:T(8,128)}) %all-gather.5.cloned.1.call-update) | async-done | bytes 5242896 | tf_op jit(solution)/shard_map/all_gather | solution.py:50
  509.3 12.1 %gather_fusion.1 = f32[120,128,256]{2,1,0:T(8,128)} fusion(f32[40,128,256]{2,1,0:T(8,128)} %bitcast.167, s32[1024]{0:T(1024)S(1)} %pad_clamp_fusion), kind=kCustom, calls=%fused_computation.1 | custom fusion | bytes 31457760 | tf_op jit(solution)/shard_map/gather | solution.py:52
  521.4 20.2 %convolution_bitcast_fusion = f32[120,128,256]{1,2,0:T(8,128)} fusion(f32[120,128,256]{2,1,0:T(8,128)} %gather_fusion.1, bf16[120,128,128]{2,1,0:T(8,128)(2,1)} %param.8), kind=kOutput, calls=%fused_computation.10 | convolution fusion | flops 6039797760 | bytes 35389440 | tf_op jit(solution)/shard_map/sij,sjk->sik/dot_general | solution.py:53
  541.6 15.7 %copy.42 = f32[15,8,128,256]{3,1,2,0:T(8,128)} copy(f32[15,8,128,256]{2,3,1,0:T(8,128)} %bitcast.165) | data formatting | bytes 31457280
  557.3 11.6 fusion.51
  568.9 78.6 %fusion.1 = f32[8,32768]{1,0:T(8,128)S(1)} fusion(f32[20,32768]{1,0:T(8,128)} %fusion.51), kind=kCustom, calls=%all-reduce-scatter.1 | all-reduce-scatter fusion | flops 1048577 | bytes 3670528
  647.4 2.3 collective-permute-start.2
  651.5 1.9 fusion.82
  653.4 19.9 %collective-permute-done.3 = f32[1,32768]{1,0:T(1,128)S(1)} collective-permute-done((f32[1,32768]{1,0:T(1,128)S(1)}, f32[1,32768]{1,0:T(1,128)S(1)}, u32[]{:S(2)}, u32[]{:S(2)}) %collective-permute-start.3) | collective-permute-done | bytes 131104
  673.3 21.2 %concatenate.4 = f32[17,32768]{1,0:T(8,128)} concatenate(f32[1,32768]{1,0:T(1,128)S(1)} %collective-permute-done.3, f32[8,32768]{1,0:T(8,128)} %collective-permute-done.2, f32[8,32768]{1,0:T(8,128)S(1)} %fusion.1), dimensions={0} | concatenate | bytes 4456448
  696.6 2.1 fusion.30
  698.8 131.3 %all-reduce.15.cloned.1.call-done = (f32[256,256]{0,1:T(8,128)}, f32[256,256]{1,0:T(8,128)}) async-done(((f32[256,256]{0,1:T(8,128)}, f32[256,256]{1,0:T(8,128)}), (f32[256,256]{0,1:T(8,128)}, f32[256,256]{1,0:T(8,128)})) %all-reduce.15.cloned.1.call-update) | async-done | bytes 524304 | tf_op jit(solution)/shard_map/psum | solution.py:68
  832.2 11.7 %cholesky.248 = f32[128,128]{1,0:T(8,128)S(1)} custom-call(f32[128,128]{1,0:T(8,128)S(1)} %cholesky.349), custom_call_target="Cholesky" | custom-call | tf_op jit(solution)/shard_map/jit(cholesky)/cholesky | solution.py:15
  844.0 9.8 custom-call.19
  854.3 11.7 %cholesky.265 = f32[128,128]{1,0:T(8,128)S(1)} custom-call(f32[128,128]{1,0:T(8,128)S(1)} %convolution_subtract_fusion.6), custom_call_target="Cholesky" | custom-call | tf_op jit(solution)/shard_map/jit(cholesky)/cholesky | solution.py:15
  868.7 4.0 while.9
  872.7 19.8 %custom-call.20 = f32[2,128,128]{1,2,0:T(8,128)S(1)} custom-call(f32[2,128,128]{2,1,0:T(8,128)S(1)} %get-tuple-element.31), custom_call_target="InvertDiagBlocksLowerTriangular" | custom-call | tf_op jit(solution)/shard_map/jit(_solve_triangular)/triangular_solve | solution.py:16
  895.2 11.7 %cholesky.282 = f32[128,128]{1,0:T(8,128)S(1)} custom-call(f32[128,128]{1,0:T(8,128)S(1)} %cholesky.352), custom_call_target="Cholesky" | custom-call | tf_op jit(solution)/shard_map/jit(cholesky)/cholesky | solution.py:15
  907.0 9.8 custom-call.21
  917.3 11.9 %cholesky.299 = f32[128,128]{1,0:T(8,128)S(1)} custom-call(f32[128,128]{1,0:T(8,128)S(1)} %convolution_subtract_fusion.5), custom_call_target="Cholesky" | custom-call | tf_op jit(solution)/shard_map/jit(cholesky)/cholesky | solution.py:15
  931.8 4.0 while.10
  935.8 19.7 %custom-call.22 = f32[2,128,128]{1,2,0:T(8,128)S(1)} custom-call(f32[2,128,128]{2,1,0:T(8,128)S(1)} %get-tuple-element.32), custom_call_target="InvertDiagBlocksLowerTriangular" | custom-call | tf_op jit(solution)/shard_map/jit(_solve_triangular)/triangular_solve | solution.py:16
  957.2 1.9 fusion.83
  960.3 124.6 %all-reduce.13.cloned.1.call-done = f32[256,256]{0,1:T(8,128)} async-done(((f32[256,256]{0,1:T(8,128)}), f32[256,256]{0,1:T(8,128)}) %all-reduce.13.cloned.1.call-update) | async-done | bytes 262160 | tf_op jit(solution)/shard_map/psum | solution.py:83
  1087.0 11.7 %cholesky.316 = f32[128,128]{1,0:T(8,128)S(1)} custom-call(f32[128,128]{1,0:T(8,128)S(1)} %cholesky.355), custom_call_target="Cholesky" | custom-call | tf_op jit(solution)/shard_map/jit(cholesky)/cholesky | solution.py:15
  1098.8 9.8 custom-call.23
  1109.1 11.9 %cholesky.333 = f32[128,128]{1,0:T(8,128)S(1)} custom-call(f32[128,128]{1,0:T(8,128)S(1)} %convolution_subtract_fusion.4), custom_call_target="Cholesky" | custom-call | tf_op jit(solution)/shard_map/jit(cholesky)/cholesky | solution.py:15
  1123.8 4.1 while.11
  1127.9 19.7 %custom-call.24 = f32[2,128,128]{1,2,0:T(8,128)S(1)} custom-call(f32[2,128,128]{2,1,0:T(8,128)S(1)} %get-tuple-element.33), custom_call_target="InvertDiagBlocksLowerTriangular" | custom-call | tf_op jit(solution)/shard_map/jit(_solve_triangular)/triangular_solve | solution.py:16
  (127 shorter events, 50.9 us)
Async XLA Ops:
  7.2 29.4 %copy-start.3 = (s32[120]{0:T(128)S(1)}, s32[120]{0:T(128)}, u32[]{:S(2)}) copy-start(s32[120]{0:T(128)} %param.10) | copy-start | bytes 1444
  7.2 68.7 %all-gather.3.cloned.1.call-start = ((), (), s32[]{:S(2)}) async-start(), calls=%async_computation | async-start | bytes 5898240 | tf_op jit(solution)/shard_map/all_gather | solution.py:50
  36.5 357.1 %all-reduce.11.cloned.1.call-start = ((), (), s32[]{:S(2)}) async-start(), calls=%async_computation.1 | async-start | bytes 524288 | tf_op jit(solution)/shard_map/psum | solution.py:65
  108.2 15.7 %copy-start.2 = (s32[120]{0:T(128)S(1)}, s32[120]{0:T(128)}, u32[]{:S(2)}) copy-start(s32[120]{0:T(128)} %param.9) | copy-start | bytes 1444
  212.9 49.5 %copy-start = (f32[640,256]{1,0:T(8,128)S(1)}, f32[640,256]{1,0:T(8,128)}, u32[]{:S(2)}) copy-start(f32[640,256]{1,0:T(8,128)} %param.12) | copy-start | bytes 1966084
  212.9 26.2 %collective-permute-start = (f32[8,32768]{1,0:T(8,128)}, f32[8,32768]{1,0:T(8,128)S(1)}, u32[]{:S(2)}, u32[]{:S(2)}) collective-permute-start(f32[8,32768]{1,0:T(8,128)} %fusion), channel_id=1, source_target_pairs={{0,8},{8,16},{16,24},{1,9},{9,17},{17,25},{2,10},{10,18},{18,26},{... | collective-permute-start | bytes 3145736
  215.7 23.4 %collective-permute-start.1 = (f32[1,32768]{1,0:T(1,128)S(1)}, f32[1,32768]{1,0:T(1,128)S(1)}, u32[]{:S(2)}, u32[]{:S(2)}) collective-permute-start(f32[1,32768]{1,0:T(1,128)S(1)} %slice.54), channel_id=1, source_target_pairs={{0,16},{8,24},{1,17},{9,25},{2,18},{10,26},{3,19},{11,27},{4,20},{... | collective-permute-start | bytes 393224
  264.6 244.7 %all-gather.5.cloned.1.call-start = ((), (), s32[]{:S(2)}) async-start(), calls=%async_computation.2 | async-start | bytes 5898240 | tf_op jit(solution)/shard_map/all_gather | solution.py:50
  469.1 361.0 %all-reduce.15.cloned.1.call-start = ((), (), s32[]{:S(2)}) async-start(), calls=%async_computation.4 | async-start | bytes 1048576 | tf_op jit(solution)/shard_map/psum | solution.py:68
  647.4 25.9 %collective-permute-start.2 = (f32[8,32768]{1,0:T(8,128)S(1)}, f32[8,32768]{1,0:T(8,128)}, u32[]{:S(2)}, u32[]{:S(2)}) collective-permute-start(f32[8,32768]{1,0:T(8,128)S(1)} %fusion.1), channel_id=1, source_target_pairs={{0,8},{8,16},{16,24},{1,9},{9,17},{17,25},{2,10},{10,18},{18,26},{... | collective-permute-start | bytes 3145736
  649.8 23.5 %collective-permute-start.3 = (f32[1,32768]{1,0:T(1,128)S(1)}, f32[1,32768]{1,0:T(1,128)S(1)}, u32[]{:S(2)}, u32[]{:S(2)}) collective-permute-start(f32[1,32768]{1,0:T(1,128)S(1)} %slice.55), channel_id=1, source_target_pairs={{0,16},{8,24},{1,17},{9,25},{2,18},{10,26},{3,19},{11,27},{4,20},{... | collective-permute-start | bytes 393224
  698.7 386.2 %all-reduce.13.cloned.1.call-start = ((), (), s32[]{:S(2)}) async-start(), calls=%async_computation.3 | async-start | bytes 524288 | tf_op jit(solution)/shard_map/psum | solution.py:83
  830.1 64.1 %copy-start.1 = (f32[256,256]{1,0:T(8,128)S(1)}, f32[256,256]{1,0:T(8,128)}, u32[]{:S(2)}) copy-start(f32[256,256]{1,0:T(8,128)} %get-tuple-element.67) | copy-start | bytes 786436
Sparse Core Ops, SparseCore 0:
  36.7 39.1 all-gather.2
  264.7 128.9 all-reduce.10
  469.2 40.0 all-gather.4
  698.9 131.1 all-reduce.14
  959.2 125.6 all-reduce.12
where the time goes:
time: 1170 us; the launch traced here: 1160 us
  waiting for transfers between devices  504 us (43%)
  other arithmetic  227 us (19%)
  blocking collectives  177 us (15%)
  local copies, waits for them, and re-layouts  125 us (11%)
  matrix products  82.1 us (7%)
  between operations  22.1 us (2%)
    unnamed x3, blocking collectives  177 us
    another operation x27, other arithmetic, inverse_lower(): lower = jnp.linalg.cholesky(gram)  138 us
    psum x1, waiting for transfers between devices, body(): lax.psum((local_gram(raw_image), local_gram(pending)), ('col', 'row'))  131 us
    psum x1, waiting for transfers between devices, body(): inner_gram = lax.psum(local_gram(raw_image), ('col', 'row'))  129 us
    psum x1, waiting for transfers between devices, body(): final_gram = lax.psum(local_gram(pending), ('col', 'row'))  125 us
    unnamed x17, local copies, waits for them, and re-layouts  80.2 us
    all_gather x2, waiting for transfers between devices, body(): gathered = lax.all_gather(mapped_scaled, 'row', axis=0, tiled=True)  79.4 us
    another operation x9, other arithmetic, inverse_lower(): jax.scipy.linalg.solve_triangular(lower, jnp.eye(gram.shape[0], dtype=jnp...  79 us
  transfers between devices with their start and end apart: 9, of which 7 were waited for; matrix products, arithmetic and copies ran while one was open for 0% of the time, Pallas kernels for 0%

commit v1 on v0

--- a/solution.py
+++ b/solution.py
@@ -80,7 +80,9 @@
             )
         pending = apply_factor(image_block, inverse_lower(inner_gram))
         firsts.append(pending)
-    final_gram = lax.psum(local_gram(pending), ("col", "row"))
+    final_gram = local_gram(pending)
+    for axis in ("col", "row"):
+        final_gram = lax.psum(final_gram, axis)
     basis = apply_factor(pending, inverse_lower(final_gram))
     total_images = rows_local * n_row * n_col
     root = jnp.sqrt(jnp.float32(total_images))

time: 1170 us -> 1130 us (0.966)
  waiting for transfers between devices: 504 us -> 470 us
    psum x1 -> x2, waiting for transfers between devices: 125 us -> 90.2 us  [body(): final_gram = lax.psum(final_gram, axis)]
    unnamed x9 -> x10, waiting for transfers between devices: 40 us -> 40 us
  transfers between devices with their start and end apart: 9 -> 10, of which waited for: 7 -> 8; matrix products, arithmetic and copies ran while one was open for 0% -> 0% of each run, Pallas kernels for 0% -> 0%
where the time goes in v1:
time: 1130 us; the launch traced here: 1120 us
  waiting for transfers between devices  470 us (42%)
  other arithmetic  227 us (20%)
  blocking collectives  177 us (16%)
  local copies, waits for them, and re-layouts  125 us (11%)
  matrix products  82.1 us (7%)
  between operations  22.4 us (2%)
  loops' own time  11.5 us (1%)
    unnamed x3, blocking collectives  177 us
    another operation x27, other arithmetic, inverse_lower(): lower = jnp.linalg.cholesky(gram)  138 us
    psum x1, waiting for transfers between devices, body(): lax.psum((local_gram(raw_image), local_gram(pending)), ('col', 'row'))  131 us
    psum x1, waiting for transfers between devices, body(): inner_gram = lax.psum(local_gram(raw_image), ('col', 'row'))  129 us
    psum x2, waiting for transfers between devices, body(): final_gram = lax.psum(final_gram, axis)  90.2 us
    unnamed x17, local copies, waits for them, and re-layouts  80.2 us
    all_gather x2, waiting for transfers between devices, body(): gathered = lax.all_gather(mapped_scaled, 'row', axis=0, tiled=True)  79.4 us
    another operation x9, other arithmetic, inverse_lower(): jax.scipy.linalg.solve_triangular(lower, jnp.eye(gram.shape[0], dtype=jnp...  79 us
  transfers between devices with their start and end apart: 10, of which 8 were waited for; matrix products, arithmetic and copies ran while one was open for 0% of the time, Pallas kernels for 0%

profile of v1, /device:TPU:0, one launch (start us, length us, event | category | flops | bytes accessed | tf_op | source)
XLA Modules:
  0.0 1123.0 jit_solution(1473005426352865048)
XLA Ops:
  7.9 3.2 convert_reduce_fusion
  11.9 20.4 %all-reduce.1 = f32[20,128]{1,0:T(8,128)S(1)} all-reduce(f32[20,128]{1,0:T(8,128)S(1)} %fusion.55), channel_id=2, replica_groups=mesh['col'=4,'row'=8] {'col'}, use_global_device_ids=true, to_apply=%region_1.0.clone | all-reduce | flops 2560 | bytes 20480
  34.4 2.1 broadcast_multiply_fusion.1
  36.6 39.3 %all-gather.3.cloned.1.call-done = f32[5120,256]{1,0:T(8,128)} async-done(((f32[640,256]{1,0:T(8,128)}), f32[5120,256]{1,0:T(8,128)}) %all-gather.3.cloned.1.call-update) | async-done | bytes 5242896 | tf_op jit(solution)/shard_map/all_gather | solution.py:50
  75.9 12.1 %gather_fusion = f32[120,128,256]{2,1,0:T(8,128)} fusion(f32[40,128,256]{2,1,0:T(8,128)} %bitcast.166, s32[1024]{0:T(1024)S(1)} %pad_clamp_fusion), kind=kCustom, calls=%fused_computation | custom fusion | bytes 31457760 | tf_op jit(solution)/shard_map/gather | solution.py:52
  88.0 20.2 %convolution_bitcast_fusion.1 = f32[120,128,256]{1,2,0:T(8,128)} fusion(f32[120,128,256]{2,1,0:T(8,128)} %gather_fusion, bf16[120,128,128]{2,1,0:T(8,128)(2,1)} %param.8), kind=kOutput, calls=%fused_computation.11 | convolution fusion | flops 6039797760 | bytes 35389440 | tf_op jit(solution)/shard_map/sij,sjk->sik/dot_general | solution.py:53
  108.2 15.7 %copy.41 = f32[15,8,128,256]{3,1,2,0:T(8,128)} copy(f32[15,8,128,256]{2,3,1,0:T(8,128)} %bitcast.163) | data formatting | bytes 31457280
  123.9 10.5 fusion.53
  134.4 78.5 %fusion = f32[8,32768]{1,0:T(8,128)} fusion(f32[20,32768]{1,0:T(8,128)S(1)} %fusion.53), kind=kCustom, calls=%all-reduce-scatter | all-reduce-scatter fusion | flops 1048577 | bytes 3670528
  215.7 2.6 collective-permute-start.1
  219.0 20.1 %collective-permute-done.1 = f32[1,32768]{1,0:T(1,128)S(1)} collective-permute-done((f32[1,32768]{1,0:T(1,128)S(1)}, f32[1,32768]{1,0:T(1,128)S(1)}, u32[]{:S(2)}, u32[]{:S(2)}) %collective-permute-start.1) | collective-permute-done | bytes 131104
  239.1 21.2 %concatenate.3 = f32[17,32768]{1,0:T(8,128)} concatenate(f32[1,32768]{1,0:T(1,128)S(1)} %collective-permute-done.1, f32[8,32768]{1,0:T(8,128)S(1)} %collective-permute-done, f32[8,32768]{1,0:T(8,128)} %fusion), dimensions={0} | concatenate | bytes 4456448
  262.4 2.2 fusion.29
  264.6 129.0 %all-reduce.12.cloned.1.call-done = f32[256,256]{0,1:T(8,128)} async-done(((f32[256,256]{0,1:T(8,128)}), f32[256,256]{0,1:T(8,128)}) %all-reduce.12.cloned.1.call-update) | async-done | bytes 262160 | tf_op jit(solution)/shard_map/psum | solution.py:65
  395.7 11.7 %cholesky.214 = f32[128,128]{1,0:T(8,128)S(1)} custom-call(f32[128,128]{1,0:T(8,128)S(1)} %cholesky.346), custom_call_target="Cholesky" | custom-call | tf_op jit(solution)/shard_map/jit(cholesky)/cholesky | solution.py:15
  407.5 9.8 custom-call.17
  417.8 11.7 %cholesky.231 = f32[128,128]{1,0:T(8,128)S(1)} custom-call(f32[128,128]{1,0:T(8,128)S(1)} %convolution_subtract_fusion.7), custom_call_target="Cholesky" | custom-call | tf_op jit(solution)/shard_map/jit(cholesky)/cholesky | solution.py:15
  431.8 15.1 %while.8 = (s32[]{:T(128)}, f32[256,256]{1,0:T(8,128)S(1)}, s32[2,2]{1,0:T(2,128)S(1)}, f32[2,128,128]{2,1,0:T(8,128)S(1)}, s32[]{:T(128)}) while((s32[]{:T(128)}, f32[256,256]{1,0:T(8,128)S(1)}, s32[2,2]{1,0:T(2,128)S(1)}, f32[2,128,128]{2,1,0:T(8,128)S(1)}, s32[]{:T(128)}) %tuple.83), condition=%wide.while_cond, body=%wide.while_body.sunk | while | flops 2 | bytes 131181 | solution.py:16
  446.9 19.7 %custom-call.18 = f32[2,128,128]{1,2,0:T(8,128)S(1)} custom-call(f32[2,128,128]{2,1,0:T(8,128)S(1)} %get-tuple-element.30), custom_call_target="InvertDiagBlocksLowerTriangular" | custom-call | tf_op jit(solution)/shard_map/jit(_solve_triangular)/triangular_solve | solution.py:16
  469.1 40.2 %all-gather.5.cloned.1.call-done = f32[5120,256]{1,0:T(8,128)} async-done(((f32[640,256]{1,0:T(8,128)}), f32[5120,256]{1,0:T(8,128)}) %all-gather.5.cloned.1.call-update) | async-done | bytes 5242896 | tf_op jit(solution)/shard_map/all_gather | solution.py:50
  509.3 12.1 %gather_fusion.1 = f32[120,128,256]{2,1,0:T(8,128)} fusion(f32[40,128,256]{2,1,0:T(8,128)} %bitcast.167, s32[1024]{0:T(1024)S(1)} %pad_clamp_fusion), kind=kCustom, calls=%fused_computation.1 | custom fusion | bytes 31457760 | tf_op jit(solution)/shard_map/gather | solution.py:52
  521.4 20.2 %convolution_bitcast_fusion = f32[120,128,256]{1,2,0:T(8,128)} fusion(f32[120,128,256]{2,1,0:T(8,128)} %gather_fusion.1, bf16[120,128,128]{2,1,0:T(8,128)(2,1)} %param.8), kind=kOutput, calls=%fused_computation.10 | convolution fusion | flops 6039797760 | bytes 35389440 | tf_op jit(solution)/shard_map/sij,sjk->sik/dot_general | solution.py:53
  541.6 15.7 %copy.42 = f32[15,8,128,256]{3,1,2,0:T(8,128)} copy(f32[15,8,128,256]{2,3,1,0:T(8,128)} %bitcast.165) | data formatting | bytes 31457280
  557.3 11.6 %fusion.51 = f32[20,32768]{1,0:T(8,128)} fusion(f32[120,32768]{1,0:T(8,128)} %bitcast.162, f32[120]{0:T(128)S(1)} %compare_convert_fusion, s32[120]{0:T(128)S(1)} %copy-done.2), kind=kOutput, calls=%fused_computation.109 | convolution fusion | flops 943723200 | bytes 18351040 | tf_op jit(solution)/shard_map/dot_general | solution.py:56
  568.9 78.6 %fusion.1 = f32[8,32768]{1,0:T(8,128)S(1)} fusion(f32[20,32768]{1,0:T(8,128)} %fusion.51), kind=kCustom, calls=%all-reduce-scatter.1 | all-reduce-scatter fusion | flops 1048577 | bytes 3670528
  647.4 2.3 collective-permute-start.2
  653.4 19.9 %collective-permute-done.3 = f32[1,32768]{1,0:T(1,128)S(1)} collective-permute-done((f32[1,32768]{1,0:T(1,128)S(1)}, f32[1,32768]{1,0:T(1,128)S(1)}, u32[]{:S(2)}, u32[]{:S(2)}) %collective-permute-start.3) | collective-permute-done | bytes 131104
  673.3 21.2 %concatenate.4 = f32[17,32768]{1,0:T(8,128)} concatenate(f32[1,32768]{1,0:T(1,128)S(1)} %collective-permute-done.3, f32[8,32768]{1,0:T(8,128)} %collective-permute-done.2, f32[8,32768]{1,0:T(8,128)S(1)} %fusion.1), dimensions={0} | concatenate | bytes 4456448
  696.6 2.1 fusion.30
  698.8 131.3 %all-reduce.18.cloned.1.call-done = (f32[256,256]{0,1:T(8,128)}, f32[256,256]{1,0:T(8,128)}) async-done(((f32[256,256]{0,1:T(8,128)}, f32[256,256]{1,0:T(8,128)}), (f32[256,256]{0,1:T(8,128)}, f32[256,256]{1,0:T(8,128)})) %all-reduce.18.cloned.1.call-update) | async-done | bytes 524304 | tf_op jit(solution)/shard_map/psum | solution.py:68
  832.2 11.7 %cholesky.248 = f32[128,128]{1,0:T(8,128)S(1)} custom-call(f32[128,128]{1,0:T(8,128)S(1)} %cholesky.349), custom_call_target="Cholesky" | custom-call | tf_op jit(solution)/shard_map/jit(cholesky)/cholesky | solution.py:15
  844.0 9.8 custom-call.19
  854.3 11.7 %cholesky.265 = f32[128,128]{1,0:T(8,128)S(1)} custom-call(f32[128,128]{1,0:T(8,128)S(1)} %convolution_subtract_fusion.6), custom_call_target="Cholesky" | custom-call | tf_op jit(solution)/shard_map/jit(cholesky)/cholesky | solution.py:15
  868.7 4.0 while.9
  872.7 19.8 %custom-call.20 = f32[2,128,128]{1,2,0:T(8,128)S(1)} custom-call(f32[2,128,128]{2,1,0:T(8,128)S(1)} %get-tuple-element.31), custom_call_target="InvertDiagBlocksLowerTriangular" | custom-call | tf_op jit(solution)/shard_map/jit(_solve_triangular)/triangular_solve | solution.py:16
  895.2 11.7 %cholesky.282 = f32[128,128]{1,0:T(8,128)S(1)} custom-call(f32[128,128]{1,0:T(8,128)S(1)} %cholesky.352), custom_call_target="Cholesky" | custom-call | tf_op jit(solution)/shard_map/jit(cholesky)/cholesky | solution.py:15
  907.0 9.8 custom-call.21
  917.3 11.9 %cholesky.299 = f32[128,128]{1,0:T(8,128)S(1)} custom-call(f32[128,128]{1,0:T(8,128)S(1)} %convolution_subtract_fusion.5), custom_call_target="Cholesky" | custom-call | tf_op jit(solution)/shard_map/jit(cholesky)/cholesky | solution.py:15
  931.8 4.0 while.10
  935.8 19.7 %custom-call.22 = f32[2,128,128]{1,2,0:T(8,128)S(1)} custom-call(f32[2,128,128]{2,1,0:T(8,128)S(1)} %get-tuple-element.32), custom_call_target="InvertDiagBlocksLowerTriangular" | custom-call | tf_op jit(solution)/shard_map/jit(_solve_triangular)/triangular_solve | solution.py:16
  957.2 1.9 fusion.83
  959.2 34.7 %all-reduce.14.cloned.1.call-done = f32[256,256]{0,1:T(8,128)} async-done(((f32[256,256]{0,1:T(8,128)}), f32[256,256]{0,1:T(8,128)}) %all-reduce.14.cloned.1.call-update) | async-done | bytes 262160 | tf_op jit(solution)/shard_map/psum | solution.py:85
  995.1 55.5 %all-reduce.16.cloned.1.call-done = f32[256,256]{0,1:T(8,128)} async-done(((f32[256,256]{0,1:T(8,128)}), f32[256,256]{0,1:T(8,128)}) %all-reduce.16.cloned.1.call-update) | async-done | bytes 262160 | tf_op jit(solution)/shard_map/psum | solution.py:85
  1052.6 11.7 %cholesky.316 = f32[128,128]{1,0:T(8,128)S(1)} custom-call(f32[128,128]{1,0:T(8,128)S(1)} %cholesky.355), custom_call_target="Cholesky" | custom-call | tf_op jit(solution)/shard_map/jit(cholesky)/cholesky | solution.py:15
  1064.4 9.8 custom-call.23
  1074.7 11.7 %cholesky.333 = f32[128,128]{1,0:T(8,128)S(1)} custom-call(f32[128,128]{1,0:T(8,128)S(1)} %convolution_subtract_fusion.4), custom_call_target="Cholesky" | custom-call | tf_op jit(solution)/shard_map/jit(cholesky)/cholesky | solution.py:15
  1089.2 4.4 while.11
  1093.6 19.7 %custom-call.24 = f32[2,128,128]{1,2,0:T(8,128)S(1)} custom-call(f32[2,128,128]{2,1,0:T(8,128)S(1)} %get-tuple-element.33), custom_call_target="InvertDiagBlocksLowerTriangular" | custom-call | tf_op jit(solution)/shard_map/jit(_solve_triangular)/triangular_solve | solution.py:16
  (130 shorter events, 52.8 us)
Async XLA Ops:
  7.2 29.4 %copy-start.3 = (s32[120]{0:T(128)S(1)}, s32[120]{0:T(128)}, u32[]{:S(2)}) copy-start(s32[120]{0:T(128)} %param.10) | copy-start | bytes 1444
  7.2 68.7 %all-gather.3.cloned.1.call-start = ((), (), s32[]{:S(2)}) async-start(), calls=%async_computation | async-start | bytes 5898240 | tf_op jit(solution)/shard_map/all_gather | solution.py:50
  36.5 357.1 %all-reduce.12.cloned.1.call-start = ((), (), s32[]{:S(2)}) async-start(), calls=%async_computation.1 | async-start | bytes 524288 | tf_op jit(solution)/shard_map/psum | solution.py:65
  108.2 15.7 %copy-start.2 = (s32[120]{0:T(128)S(1)}, s32[120]{0:T(128)}, u32[]{:S(2)}) copy-start(s32[120]{0:T(128)} %param.9) | copy-start | bytes 1444
  212.9 49.5 %copy-start = (f32[640,256]{1,0:T(8,128)S(1)}, f32[640,256]{1,0:T(8,128)}, u32[]{:S(2)}) copy-start(f32[640,256]{1,0:T(8,128)} %param.12) | copy-start | bytes 1966084
  212.9 26.2 %collective-permute-start = (f32[8,32768]{1,0:T(8,128)}, f32[8,32768]{1,0:T(8,128)S(1)}, u32[]{:S(2)}, u32[]{:S(2)}) collective-permute-start(f32[8,32768]{1,0:T(8,128)} %fusion), channel_id=1, source_target_pairs={{0,8},{8,16},{16,24},{1,9},{9,17},{17,25},{2,10},{10,18},{18,26},{... | collective-permute-start | bytes 3145736
  215.7 23.4 %collective-permute-start.1 = (f32[1,32768]{1,0:T(1,128)S(1)}, f32[1,32768]{1,0:T(1,128)S(1)}, u32[]{:S(2)}, u32[]{:S(2)}) collective-permute-start(f32[1,32768]{1,0:T(1,128)S(1)} %slice.54), channel_id=1, source_target_pairs={{0,16},{8,24},{1,17},{9,25},{2,18},{10,26},{3,19},{11,27},{4,20},{... | collective-permute-start | bytes 393224
  264.6 244.7 %all-gather.5.cloned.1.call-start = ((), (), s32[]{:S(2)}) async-start(), calls=%async_computation.2 | async-start | bytes 5898240 | tf_op jit(solution)/shard_map/all_gather | solution.py:50
  469.1 361.0 %all-reduce.18.cloned.1.call-start = ((), (), s32[]{:S(2)}) async-start(), calls=%async_computation.5 | async-start | bytes 1048576 | tf_op jit(solution)/shard_map/psum | solution.py:68
  647.4 25.9 %collective-permute-start.2 = (f32[8,32768]{1,0:T(8,128)S(1)}, f32[8,32768]{1,0:T(8,128)}, u32[]{:S(2)}, u32[]{:S(2)}) collective-permute-start(f32[8,32768]{1,0:T(8,128)S(1)} %fusion.1), channel_id=1, source_target_pairs={{0,8},{8,16},{16,24},{1,9},{9,17},{17,25},{2,10},{10,18},{18,26},{... | collective-permute-start | bytes 3145736
  649.8 23.5 %collective-permute-start.3 = (f32[1,32768]{1,0:T(1,128)S(1)}, f32[1,32768]{1,0:T(1,128)S(1)}, u32[]{:S(2)}, u32[]{:S(2)}) collective-permute-start(f32[1,32768]{1,0:T(1,128)S(1)} %slice.55), channel_id=1, source_target_pairs={{0,16},{8,24},{1,17},{9,25},{2,18},{10,26},{3,19},{11,27},{4,20},{... | collective-permute-start | bytes 393224
  698.7 295.1 %all-reduce.14.cloned.1.call-start = ((), (), s32[]{:S(2)}) async-start(), calls=%async_computation.3 | async-start | bytes 524288 | tf_op jit(solution)/shard_map/psum | solution.py:85
  830.1 64.1 %copy-start.1 = (f32[256,256]{1,0:T(8,128)S(1)}, f32[256,256]{1,0:T(8,128)}, u32[]{:S(2)}) copy-start(f32[256,256]{1,0:T(8,128)} %get-tuple-element.67) | copy-start | bytes 786436
  959.1 91.4 %all-reduce.16.cloned.1.call-start = ((), (), s32[]{:S(2)}) async-start(), calls=%async_computation.4 | async-start | bytes 524288 | tf_op jit(solution)/shard_map/psum | solution.py:85
Sparse Core Ops, SparseCore 0:
  36.7 39.1 all-gather.2
  264.7 128.9 all-reduce.11
  469.2 40.0 all-gather.4
  698.9 131.1 all-reduce.17
  959.2 34.5 all-reduce.13
  996.8 53.7 all-reduce.15
